TPU v7x, 256 devices: a whole 4x4x8 slice. The times are simulated.
256 devices in a mesh: br: 64 (over z, y_hi, x), bus: 4 (over y_lo, core).
Axes of the slice: x: 4, y: 4 (y_hi: 2, y_lo: 2; y = y_hi * 2 + y_lo), z: 8, core: 2. Of those that a mesh axis runs over, the one named last changes fastest.
Arguments:
- net_load: bfloat16 [128, 60416], P('br', 'bus'), may hold values from -6 to 6
- release: float32 [128, 1024], P('br'), may hold values from 0 to 2
- plant_bus: int32 [1024], replicated, may hold values from 0 to 60415
- efficiency: float32 [1024], replicated, may hold values from 0.5 to 2
- ptdf: bfloat16 [8192, 60416], P('br', 'bus'), may hold values from -0.0234375 to 0.0234375
- branch_class: int32 [8192], P('br'), may hold values from 0 to 15
- class_limit: float32 [16], replicated, may hold values from 0.4 to 3
- class_price: float32 [16], replicated, may hold values from 0.5 to 5
Outputs:
- grad_bus: float32 [128, 60416], P('br', 'bus')
- grad_release: float32 [128, 1024], P('br')
All inputs are finite; a program needn't handle non-finite values.
Results may differ from a plain program's by a relative error of at most 0.0031.
Values may be sent and summed in bfloat16 or wider, within the bound.
A program may use at most 64 MiB of HBM per device.

v0:
```python
import jax
import jax.numpy as jnp
from jax import lax
from jax.sharding import PartitionSpec as P

SMOOTH = 0.25


def shards(net_load, release, plant_bus, efficiency, ptdf, branch_class, class_limit, class_price):
    rows_local, bus_local = net_load.shape
    offset = lax.axis_index("bus") * bus_local
    columns = plant_bus - offset
    inside = ((columns >= 0) & (columns < bus_local)).astype(jnp.float32)
    clipped = jnp.clip(columns, 0, bus_local - 1)
    weighted = efficiency * inside
    inject = (
        net_load.astype(jnp.float32)
        .at[:, clipped]
        .add(release * weighted[None, :])
        .astype(jnp.bfloat16)
    )
    partial_flows = lax.dot_general(
        lax.all_gather(inject, "br", axis=0, tiled=True),
        ptdf,
        (((1,), (1,)), ((), ())),
        preferred_element_type=jnp.float32,
    )
    onehot = (branch_class[:, None] == jnp.arange(class_limit.shape[0])[None, :]).astype(
        jnp.float32
    )
    limit = jnp.sum(onehot * class_limit[None, :], axis=1)[None, :]
    price = jnp.sum(onehot * class_price[None, :], axis=1)[None, :]
    flows = lax.psum(partial_flows, "bus")
    upper = jax.nn.sigmoid((flows - limit) / SMOOTH)
    lower = jax.nn.sigmoid((-flows - limit) / SMOOTH)
    grad_flow = (price * (upper - lower)).astype(jnp.bfloat16)
    grad_bus = lax.psum_scatter(
        jnp.dot(grad_flow, ptdf, preferred_element_type=jnp.float32),
        "br",
        scatter_dimension=0,
        tiled=True,
    )
    picked = grad_bus[:, clipped] * weighted[None, :]
    grad_release = lax.psum(picked, "bus")
    return (grad_bus, grad_release)


def solution(mesh):
    placed = (P("br", "bus"), P("br", None), P(), P(), P("br", "bus"), P("br"), P(), P())
    return jax.shard_map(
        shards,
        mesh=mesh,
        in_specs=placed,
        out_specs=(P("br", "bus"), P("br", None)),
        check_vma=False,
    )
```

profile of v0, /device:TPU:1, one launch (start us, length us, event | category | flops | bytes accessed | tf_op | source)
XLA Modules:
  0.0 980.8 jit_solution(10808538749008123875)
XLA Ops:
  7.2 0.0 all-gather.3.cloned.1.call-start
  7.2 0.7 broadcast_clamp_fusion
  7.9 0.7 and_select_fusion
  8.6 0.7 multiply_bitcast_fusion.1
  9.3 0.2 copy.25
  9.6 4.7 copy.24
  14.3 11.7 %scatter_fusion = f32[2,15104]{0,1:T(8,128)} fusion(f32[2,15104]{0,1:T(8,128)} %copy.24, s32[1024]{0:T(1024)S(1)} %get-tuple-element.13, f32[1024,2]{1,0:T(8,128)S(1)} %copy.25), kind=kCustom, calls=%fused_computation.1 | custom fusion | flops 2048 | bytes 28672 | tf_op jit(solution)/shard_map/scatter-add | solution.py:19
  26.0 4.7 convert_bitcast_fusion
  30.7 4.1 copy.26
  34.9 0.0 all-gather.3.cloned.1.call-update
  34.9 0.0 all-reduce.4.cloned.1.call-start
  34.9 126.9 %all-gather.3.cloned.1.call-done = bf16[64,2,15104]{2,1,0:T(2,128)(2,1)} async-done(((bf16[1,2,15104]{2,1,0:T(2,128)(2,1)}), bf16[64,2,15104]{2,1,0:T(2,128)(2,1)}) %all-gather.3.cloned.1.call-update) | async-done | bytes 3866640 | tf_op jit(solution)/shard_map/all_gather | solution.py:23
  161.8 8.2 reshape.29
  170.0 5.1 fusion.7
  175.1 0.0 all-reduce.4.cloned.1.call-update
  175.1 0.0 all-reduce.6.cloned.1.call-start
  175.2 0.0 copy-done.1
  175.2 0.0 copy-done.2
  175.2 0.1 select_reduce_fusion.1
  175.3 40.9 %all-reduce.4.cloned.1.call-done = f32[128,128]{1,0:T(8,128)} async-done(((f32[128,128]{1,0:T(8,128)}), f32[128,128]{1,0:T(8,128)}) %all-reduce.4.cloned.1.call-update) | async-done | bytes 65552 | tf_op jit(solution)/shard_map/psum | solution.py:33
  216.2 6.4 fusion
  222.5 0.0 all-reduce.6.cloned.1.call-update
  222.6 0.6 copy-done.4
  223.2 0.6 dynamic-slice
  224.5 681.8 %all-reduce.6.cloned.1.call-done = f32[128,15104]{1,0:T(8,128)} async-done(((f32[128,15104]{1,0:T(8,128)}), f32[128,15104]{1,0:T(8,128)}) %all-reduce.6.cloned.1.call-update) | async-done | bytes 7733264
  906.2 1.1 constant_dynamic-slice_fusion
  907.3 0.0 copy-start
  907.3 4.7 copy.27
  912.0 6.0 gather_fusion
  918.0 0.2 multiply_bitcast_fusion
  918.3 55.2 %psum.15 = f32[2,1024]{0,1:T(8,128)S(1)} all-reduce(f32[2,1024]{0,1:T(8,128)S(1)} %multiply_bitcast_fusion), channel_id=1, replica_groups=mesh['br'=64,'bus'=4] {'bus'}, use_global_device_ids=true, to_apply=%region_5.6 | all-reduce | flops 2048 | bytes 16384 | tf_op jit(solution)/shard_map/psum | solution.py:44
  973.5 0.8 copy.28
  (6 shorter events, 0.0 us)
Async XLA Ops:
  7.2 154.6 %all-gather.3.cloned.1.call-start = ((), (), s32[]{:S(2)}) async-start(), calls=%async_computation.1 | async-start | bytes 3927040 | tf_op jit(solution)/shard_map/all_gather | solution.py:23
  34.9 181.3 %all-reduce.4.cloned.1.call-start = ((), (), s32[]{:S(2)}) async-start(), calls=%async_computation | async-start | bytes 131072 | tf_op jit(solution)/shard_map/psum | solution.py:33
  170.0 5.2 copy-start.1
  170.0 5.2 copy-start.2
  170.0 5.2 copy-start.3
  175.1 731.1 %all-reduce.6.cloned.1.call-start = ((), (), s32[]{:S(2)}) async-start(), calls=%async_computation.2 | async-start | bytes 15466496
  222.5 0.7 copy-start.4
  907.3 4.7 copy-start
Sparse Core Ops, SparseCore 0:
  35.0 126.7 all-gather.2
  175.3 40.8 all-reduce.3
  222.7 683.4 all-reduce.5
where the time goes:
time: 981 us
  waiting for transfers between devices  850 us (87%)
  blocking collectives  55.2 us (6%)
  local copies, waits for them, and re-layouts  31.2 us (3%)
  other arithmetic  18.8 us (2%)
  between operations  14.5 us (1%)
  matrix products  11.5 us (1%)
    unnamed x4, waiting for transfers between devices  682 us
    all_gather x1, waiting for transfers between devices, shards(): lax.all_gather(inject, 'br', axis=0, tiled=True)  127 us
    psum x1, blocking collectives, shards(): grad_release = lax.psum(picked, 'bus')  55.2 us
    psum x1, waiting for transfers between devices, shards(): flows = lax.psum(partial_flows, 'bus')  40.9 us
  transfers between devices with their start and end apart: 3, of which 3 were waited for; matrix products, arithmetic and copies ran while one was open for 0% of the time, Pallas kernels for 0%

commit v1 on v0

v1 whole, which is shorter than its diff:
```python
import functools

import jax
import jax.numpy as jnp
from jax import lax
from jax.experimental import pallas as pl
from jax.experimental.pallas import tpu as pltpu
from jax.sharding import PartitionSpec as P

SMOOTH = 0.25
LANES = 128
NX, NY, NZ = 4, 2, 8
MESH = pl.DeviceIdType.MESH
NT = (((1,), (1,)), ((), ()))
TN = (((0,), (0,)), ((), ()))
NN = (((1,), (0,)), ((), ()))


def mm(a, b, dims):
    return lax.dot_general(a, b, dims, preferred_element_type=jnp.float32)


def split3(v):
    one = v.astype(jnp.bfloat16)
    rest = v - one.astype(jnp.float32)
    two = rest.astype(jnp.bfloat16)
    three = (rest - two.astype(jnp.float32)).astype(jnp.bfloat16)
    return one, two, three


def kernel(
    sizes,
    net_ref, rel_ref, plant_ref, eff_ref, ptdf_ref, cls_ref, lim_ref, price_ref,
    gbus_ref, grel_ref,
    inj, acc, px, py, recv_in, xall, fpart, frecv, ftot, gx, gy, gpart, ring, sbuf, srecv, rows, prel,
    s_p, r_p, l_p, s_i, r_i, l_i, s_z, r_z, s_f, r_f, s_b, r_b, s_g, r_g, s_r, r_r, s_s, r_s, s_o, r_o,
):
    tiles, tx, ty, nbus, plants, classes = sizes
    wx, wy = tx * LANES, ty * LANES
    base_y = NX * wx
    width = wx + wy
    c0 = (width // LANES) // 2 * LANES
    chunks = ((0, c0), (c0, width - c0))
    br, bus = lax.axis_index("br"), lax.axis_index("bus")
    z, y, x = br // (NX * NY), (br // NX) % NY, br % NX
    me = y * NX + x

    def at(z_, y_, x_):
        return ((z_ * NY + y_) * NX + x_, bus)

    xy_offsets = [(dy, dx) for dy in range(NY) for dx in range(NX) if (dy, dx) != (0, 0)]

    def xy(dy, dx):
        return (y + dy) % NY, (x + dx) % NX

    zup, zdn = (z + 1) % NZ, (z + NZ - 1) % NZ
    partners = [at(z, *xy(dy, dx)) for dy, dx in xy_offsets]
    partners += [at(zup, y, x), at(zdn, y, x)]
    partners += [(br, (bus + d) % nbus) for d in range(1, nbus)]

    barrier = pltpu.get_barrier_semaphore()
    for p in partners:
        pl.semaphore_signal(barrier, inc=1, device_id=p, device_id_type=MESH)

    sends = []

    def send(src, dst, ss, rs, dev):
        c = pltpu.make_async_remote_copy(
            src_ref=src, dst_ref=dst, send_sem=ss, recv_sem=rs, device_id=dev, device_id_type=MESH
        )
        c.start()
        sends.append(c)
        return c

    def window_x(ref, q):
        return ref.at[:, pl.ds(pl.multiple_of(q * wx, LANES), wx)]

    def window_y(ref, q):
        return ref.at[:, pl.ds(pl.multiple_of(base_y + q * wy, LANES), wy)]

    own_px = pltpu.make_async_copy(window_x(ptdf_ref, x), px.at[x], l_p.at[0])
    own_py = pltpu.make_async_copy(window_y(ptdf_ref, y), py.at[y], l_p.at[1])
    own_px.start()
    own_py.start()
    pl.semaphore_wait(barrier, len(partners))

    col = plant_ref[...] - bus * (tiles * LANES)
    hi = col >> 7
    lo = col & 127
    row_id = lax.broadcasted_iota(jnp.int32, (2 * tiles, plants), 0)
    lo_id = lax.broadcasted_iota(jnp.int32, (LANES, plants), 0)
    lo_hot = (lo_id == lo).astype(jnp.float32).astype(jnp.bfloat16)
    eff = eff_ref[...]
    weight = rel_ref[...] * eff
    here = (row_id >> 1) == hi
    odd = (row_id & 1) == 1
    total = None
    for part in split3(weight):
        part = part.astype(jnp.float32)
        placed = jnp.where(here, jnp.where(odd, part[1:2, :], part[0:1, :]), 0.0)
        term = mm(placed.astype(jnp.bfloat16), lo_hot, NT)
        total = term if total is None else total + term
    acc[...] = total
    for h in range(tiles):
        cols = slice(h * LANES, (h + 1) * LANES)
        inj[:, cols] = (acc[2 * h : 2 * h + 2, :] + net_ref[:, cols].astype(jnp.float32)).astype(jnp.bfloat16)

    arrivals = []
    for k, (dy, dx) in enumerate(xy_offsets):
        y_, x_ = xy(dy, dx)
        dev = at(z, y_, x_)
        arrivals.append(send(window_x(inj, x_), recv_in.at[me, :, pl.ds(0, wx)], s_i.at[2 * k], r_i.at[2 * k], dev))
        arrivals.append(send(window_y(inj, y_), recv_in.at[me, :, pl.ds(wx, wy)], s_i.at[2 * k + 1], r_i.at[2 * k + 1], dev))
    own_ix = pltpu.make_async_copy(window_x(inj, x), recv_in.at[me, :, pl.ds(0, wx)], l_i.at[0])
    own_iy = pltpu.make_async_copy(window_y(inj, y), recv_in.at[me, :, pl.ds(wx, wy)], l_i.at[1])
    own_ix.start()
    own_iy.start()

    factor = []
    for k in range(1, NX):
        x_ = (x + k) % NX
        factor.append(send(window_x(ptdf_ref, x_), px.at[x], s_p.at[k - 1], r_p.at[k - 1], at(z, y, x_)))
    y_ = (y + 1) % NY
    factor.append(send(window_y(ptdf_ref, y_), py.at[y], s_p.at[NX - 1], r_p.at[NX - 1], at(z, y_, x)))

    cls = cls_ref[...]
    limit = jnp.zeros(cls.shape, jnp.float32)
    price = jnp.zeros(cls.shape, jnp.float32)
    for k in range(classes):
        limit = jnp.where(cls == k, lim_ref[k], limit)
        price = jnp.where(cls == k, price_ref[k], price)

    own_ix.wait()
    own_iy.wait()
    for c in arrivals:
        c.wait_recv()
    for i in range(NX * NY):
        xall[z, 2 * i : 2 * i + 2, :] = recv_in[i]

    def ring_gather(step, d, c):
        start, size = chunks[c]
        n = (z + NZ - (step - 1)) % NZ if d == 0 else (z + (step - 1)) % NZ
        block = xall.at[n, :, pl.ds(start, size)]
        return send(block, block, s_z.at[d, step - 1, c], r_z.at[d, step - 1, c], at(zup if d == 0 else zdn, y, x))

    flight = {}
    for step in range(1, NZ // 2 + 1):
        for c in range(2):
            for d in range(2):
                if step == NZ // 2 and c != d:
                    continue
                if step > 1:
                    flight[step - 1, d, c].wait_recv()
                flight[step, d, c] = ring_gather(step, d, c)
    half = NZ // 2
    flight[half - 1, 0, 1].wait_recv()
    flight[half - 1, 1, 0].wait_recv()
    for d in range(2):
        flight[half, d, d].wait_recv()

    own_px.wait()
    own_py.wait()
    for c in factor:
        c.wait_recv()
    scen = NZ * 2 * NX * NY
    lhs_x = xall[:, :, 0:wx].reshape(scen, wx)
    for q in range(NX):
        fpart[q] = mm(lhs_x, px[q], NT)
    lhs_y = xall[:, :, wx:width].reshape(scen, wy)
    for q in range(NY):
        fpart[NX + q] = mm(lhs_y, py[q], NT)

    back = []
    for k in range(1, NX):
        x_ = (x + k) % NX
        back.append(send(fpart.at[x_], frecv.at[k - 1], s_f.at[k - 1], r_f.at[k - 1], at(z, y, x_)))
    back.append(send(fpart.at[NX + y_], frecv.at[NX - 1], s_f.at[NX - 1], r_f.at[NX - 1], at(z, y_, x)))
    own = fpart[x] + fpart[NX + y]
    for k, c in enumerate(back):
        c.wait_recv()
        own = own + frecv[k]
    ftot[bus] = own
    over = []
    for d in range(1, nbus):
        over.append(send(ftot.at[bus], ftot.at[bus], s_b.at[d - 1], r_b.at[d - 1], (br, (bus + d) % nbus)))
    for c in over:
        c.wait_recv()
    flows = ftot[0]
    for b in range(1, nbus):
        flows = flows + ftot[b]
    upper = jax.nn.sigmoid((flows - limit) / SMOOTH)
    lower = jax.nn.sigmoid((-flows - limit) / SMOOTH)
    grad_flow = (price * (upper - lower)).astype(jnp.bfloat16)
    gx[x] = grad_flow
    gy[y] = grad_flow
    given = []
    for k in range(1, NX):
        x_ = (x + k) % NX
        given.append(send(gx.at[x], gx.at[x], s_g.at[k - 1], r_g.at[k - 1], at(z, y, x_)))
    given.append(send(gy.at[y], gy.at[y], s_g.at[NX - 1], r_g.at[NX - 1], at(z, y_, x)))
    for c in given:
        c.wait_recv()

    grad = mm(gx[0], px[0], NN)
    for q in range(1, NX):
        grad = grad + mm(gx[q], px[q], NN)
    gpart[:, :, 0:wx] = grad.reshape(NZ, scen // NZ, wx)
    grad = mm(gy[0], py[0], NN)
    for q in range(1, NY):
        grad = grad + mm(gy[q], py[q], NN)
    gpart[:, :, wx:width] = grad.reshape(NZ, scen // NZ, wy)

    down = {}
    for step in range(1, half + 1):
        for c in range(2):
            start, size = chunks[c]
            for d in range(2):
                if step == 1 and c != d:
                    continue
                away = half + 1 - step
                target = (z + away) % NZ if d == 0 else (z + NZ - away) % NZ
                value = gpart[target, :, start : start + size]
                if (step - 1, d, c) in down:
                    down[step - 1, d, c].wait_recv()
                    value = value + ring[1, d, step - 2, :, start : start + size].astype(jnp.float32)
                ring[0, d, step - 1, :, start : start + size] = value.astype(jnp.bfloat16)
                down[step, d, c] = send(
                    ring.at[0, d, step - 1, :, pl.ds(start, size)],
                    ring.at[1, d, step - 1, :, pl.ds(start, size)],
                    s_r.at[d, step - 1, c], r_r.at[d, step - 1, c],
                    at(zup if d == 0 else zdn, y, x),
                )
    for c in range(2):
        start, size = chunks[c]
        value = gpart[z, :, start : start + size]
        for d in range(2):
            down[half, d, c].wait_recv()
            value = value + ring[1, d, half - 1, :, start : start + size].astype(jnp.float32)
        for i in range(NX * NY):
            sbuf[i, :, start : start + size] = value[2 * i : 2 * i + 2, :]
    last = []
    for k, (dy, dx) in enumerate(xy_offsets):
        y2, x2 = xy(dy, dx)
        last.append(send(sbuf.at[y2 * NX + x2], srecv.at[me], s_s.at[k], r_s.at[k], at(z, y2, x2)))
    srecv[me] = sbuf[me]
    for c in last:
        c.wait_recv()
    for q in range(NX):
        part = srecv[q, :, 0:wx]
        for j in range(1, NY):
            part = part + srecv[j * NX + q, :, 0:wx]
        gbus_ref[:, q * wx : (q + 1) * wx] = part
    for q in range(NY):
        part = srecv[q * NX, :, wx:width]
        for j in range(1, NX):
            part = part + srecv[q * NX + j, :, wx:width]
        gbus_ref[:, base_y + q * wy : base_y + (q + 1) * wy] = part

    for h in range(tiles):
        rows[2 * h : 2 * h + 2, :] = gbus_ref[:, h * LANES : (h + 1) * LANES]
    parts = split3(rows[...])
    lo_mask = lo_id == lo
    for s in range(2):
        hot = jnp.where(here & (odd == (s == 1)), 1.0, 0.0).astype(jnp.bfloat16)
        picked = mm(parts[0], hot, TN) + mm(parts[1], hot, TN) + mm(parts[2], hot, TN)
        picked = jnp.sum(jnp.where(lo_mask, picked, 0.0), axis=0, keepdims=True)
        prel[bus, s : s + 1, :] = picked * eff
    release = []
    for d in range(1, nbus):
        release.append(send(prel.at[bus], prel.at[bus], s_o.at[d - 1], r_o.at[d - 1], (br, (bus + d) % nbus)))
    for c in release:
        c.wait_recv()
    out = prel[0]
    for b in range(1, nbus):
        out = out + prel[b]
    grel_ref[...] = out
    for c in sends:
        c.wait_send()


def shards(net_load, release, plant_bus, efficiency, ptdf, branch_class, class_limit, class_price):
    nbus = 4
    plants = plant_bus.shape[0]
    classes = class_limit.shape[0]
    branches, columns = ptdf.shape
    tiles = columns // LANES
    tx = 15
    ty = (tiles - NX * tx) // NY
    wx, wy = tx * LANES, ty * LANES
    width = wx + wy
    group = NX * NY
    scen = NZ * group * 2
    bf, f32 = jnp.bfloat16, jnp.float32
    dma = pltpu.SemaphoreType.DMA
    vmem = pl.BlockSpec(memory_space=pltpu.VMEM)
    smem = pl.BlockSpec(memory_space=pltpu.SMEM)
    return pl.pallas_call(
        functools.partial(kernel, (tiles, tx, ty, nbus, plants, classes)),
        out_shape=(
            jax.ShapeDtypeStruct((2, columns), f32),
            jax.ShapeDtypeStruct((2, plants), f32),
        ),
        in_specs=[vmem, vmem, vmem, vmem, pl.BlockSpec(memory_space=pl.ANY), vmem, smem, smem],
        out_specs=(vmem, vmem),
        scratch_shapes=[
            pltpu.VMEM((2, columns), bf),
            pltpu.VMEM((2 * tiles, LANES), f32),
            pltpu.VMEM((NX, branches, wx), bf),
            pltpu.VMEM((NY, branches, wy), bf),
            pltpu.VMEM((group, 2, width), bf),
            pltpu.VMEM((NZ, 2 * group, width), bf),
            pltpu.VMEM((NX + NY, scen, branches), f32),
            pltpu.VMEM((NX, scen, branches), f32),
            pltpu.VMEM((nbus, scen, branches), f32),
            pltpu.VMEM((NX, scen, branches), bf),
            pltpu.VMEM((NY, scen, branches), bf),
            pltpu.VMEM((NZ, 2 * group, width), f32),
            pltpu.VMEM((2, 2, NZ // 2, 2 * group, width), bf),
            pltpu.VMEM((group, 2, width), f32),
            pltpu.VMEM((group, 2, width), f32),
            pltpu.VMEM((2 * tiles, LANES), f32),
            pltpu.VMEM((nbus, 2, plants), f32),
            dma((NX,)), dma((NX,)), dma((2,)),
            dma((2 * (group - 1),)), dma((2 * (group - 1),)), dma((2,)),
            dma((2, NZ // 2, 2)), dma((2, NZ // 2, 2)),
            dma((NX,)), dma((NX,)),
            dma((nbus - 1,)), dma((nbus - 1,)),
            dma((NX,)), dma((NX,)),
            dma((2, NZ // 2, 2)), dma((2, NZ // 2, 2)),
            dma((group - 1,)), dma((group - 1,)),
            dma((nbus - 1,)), dma((nbus - 1,)),
        ],
        compiler_params=pltpu.CompilerParams(
            collective_id=0, has_side_effects=True, vmem_limit_bytes=56 << 20
        ),
    )(
        net_load,
        release,
        plant_bus[None, :],
        efficiency[None, :],
        ptdf,
        branch_class[None, :],
        class_limit,
        class_price,
    )


def solution(mesh):
    placed = (P("br", "bus"), P("br", None), P(), P(), P("br", "bus"), P("br"), P(), P())
    return jax.shard_map(
        shards,
        mesh=mesh,
        in_specs=placed,
        out_specs=(P("br", "bus"), P("br", None)),
        check_vma=False,
    )
```

time: 981 us -> 93.4 us (0.10)
  waiting for transfers between devices: 850 us -> 0 us
  Pallas kernels: 0 us -> 89.7 us
  blocking collectives: 55.2 us -> 0 us
  local copies, waits for them, and re-layouts: 31.2 us -> 2.85 us
  other arithmetic: 18.8 us -> 0 us
  between operations: 14.5 us -> 0.64 us
  matrix products: 11.5 us -> 0 us
    unnamed x4 -> x0, waiting for transfers between devices: 682 us -> none
    all_gather x1 -> x0, waiting for transfers between devices: 127 us -> none  [shards(): lax.all_gather(inject, 'br', axis=0, tiled=True)]
    pallas_call x0 -> x1, Pallas kernels: none -> 89.7 us  [shards(): pl.pallas_call(functools.partial(kernel, (tiles, tx, ty, nbus, plants, cl...]
    psum x1 -> x0, blocking collectives: 55.2 us -> none  [shards(): grad_release = lax.psum(picked, 'bus')]
    psum x1 -> x0, waiting for transfers between devices: 40.9 us -> none  [shards(): flows = lax.psum(partial_flows, 'bus')]
    unnamed x15 -> x2, local copies, waits for them, and re-layouts: 15.5 us -> 2.85 us
    scatter-add x1 -> x0, other arithmetic: 11.7 us -> none  [shards(): inject = net_load.astype(jnp.float32).at[:, clipped].add(release * weight...]
    dot_general x2 -> x0, matrix products: 11.5 us -> none  [the longest x1 6.37 us: shards(): jnp.dot(grad_flow, ptdf, preferred_element_type=jnp.float32)]
  transfers between devices with their start and end apart: 3 -> 0, of which waited for: 3 -> 0; matrix products, arithmetic and copies ran while one was open for 0% -> 0% of each run, Pallas kernels for 0% -> 0%
where the time goes in v1:
time: 93.4 us; the launch traced here: 93.2 us
  Pallas kernels  89.7 us (96%)
  local copies, waits for them, and re-layouts  2.85 us (3%)
    pallas_call x1, Pallas kernels, shards(): pl.pallas_call(functools.partial(kernel, (tiles, tx, ty, nbus, plants, cl...  89.7 us
    unnamed x2, local copies, waits for them, and re-layouts  2.85 us

profile of v1, /device:TPU:1, one launch (start us, length us, event | category | flops | bytes accessed | tf_op | source)
XLA Modules:
  0.0 93.2 jit_solution(14530230400804043699)
XLA Ops:
  0.6 89.7 %shard_map.95 = (f32[2,15104]{1,0:T(2,128)}, f32[2,1024]{1,0:T(2,128)}) custom-call(bf16[2,15104]{1,0:T(2,128)(2,1)} %net_ref.1, f32[2,1024]{1,0:T(2,128)} %rel_ref.1, s32[1,1024]{1,0:T(1,128)} %bitcast.3, f32[1,1024]{1,0:T(1,128)} %bitcast.4, bf16[128,15104]{1,0:T(8,128)(2,1)} %ptdf_ref.1, s32[1,128]{1,0:T(1,128)} %bitcast.5, f32[16]{0:T(128)} %lim_ref.1, ...), custom_call_target="tpu_custom_call" | custom-call | tf_op jit(solution)/shard_map/pallas_call | solution.py:297
  90.4 1.6 %copy.12 = f32[2,15104]{1,0:T(2,128)} copy(f32[2,15104]{1,0:T(2,128)} %get-tuple-element.4) | data formatting | bytes 241664
  91.9 1.3 %copy.13 = f32[2,1024]{1,0:T(2,128)} copy(f32[2,1024]{1,0:T(2,128)} %get-tuple-element.5) | data formatting | bytes 16384

commit v2 on v1

v2 whole, which is shorter than its diff:
```python
import functools

import jax
import jax.numpy as jnp
from jax import lax
from jax.experimental import pallas as pl
from jax.experimental.pallas import tpu as pltpu
from jax.sharding import PartitionSpec as P

SMOOTH = 0.25
LANES = 128
NX, NY, NZ = 4, 2, 8
PIECES = 4
MESH = pl.DeviceIdType.MESH
NT = (((1,), (1,)), ((), ()))
TN = (((0,), (0,)), ((), ()))
NN = (((1,), (0,)), ((), ()))


def mm(a, b, dims):
    return lax.dot_general(a, b, dims, preferred_element_type=jnp.float32)


def split3(v):
    one = v.astype(jnp.bfloat16)
    rest = v - one.astype(jnp.float32)
    two = rest.astype(jnp.bfloat16)
    three = (rest - two.astype(jnp.float32)).astype(jnp.bfloat16)
    return one, two, three


def kernel(
    sizes,
    net_ref, rel_ref, plant_ref, eff_ref, ptdf_ref, cls_ref, lim_ref, price_ref,
    gbus_ref, grel_ref,
    inj, acc, px, py, recv_in, xall, fpart, frecv, gx, gy, gpart, ring, sbuf, srecv, rows, prel, hot,
    s_p, r_p, l_p, s_i, r_i, l_i, s_z, r_z, s_f, r_f, s_g, r_g, s_r, r_r, s_s, r_s, s_o, r_o,
):
    tiles, tx, ty, nbus, plants, classes = sizes
    wx, wy = tx * LANES, ty * LANES
    base_y = NX * wx
    width = wx + wy
    part_rows = 2 * NZ * NX * NY // nbus
    third = (ty + 2) // 3 * LANES
    chunks = ((0, wx), (wx, third), (wx + third, third), (wx + 2 * third, wy - 2 * third))
    way = (0, 1, 1, 0)
    br, bus = lax.axis_index("br"), lax.axis_index("bus")
    z, y, x = br // (NX * NY), (br // NX) % NY, br % NX
    me = y * NX + x

    def at(z_, y_, x_):
        return ((z_ * NY + y_) * NX + x_, bus)

    xy_offsets = [(dy, dx) for dy in range(NY) for dx in range(NX) if (dy, dx) != (0, 0)]

    def xy(dy, dx):
        return (y + dy) % NY, (x + dx) % NX

    zup, zdn = (z + 1) % NZ, (z + NZ - 1) % NZ
    partners = [at(z, *xy(dy, dx)) for dy, dx in xy_offsets]
    partners += [at(zup, y, x), at(zdn, y, x)]
    partners += [(br, (bus + d) % nbus) for d in range(1, nbus)]
    yother = (y + 1) % NY
    holders = [(z, y, (x + k) % NX) for k in range(1, NX)] + [(z, yother, x), (z, y, x)]

    def across(j, d):
        z_, y_, x_ = holders[j]
        return ((z_ * NY + y_) * NX + x_, (bus + d) % nbus)

    partners += [across(j, d) for j in range(NX) for d in range(1, nbus)]

    barrier = pltpu.get_barrier_semaphore()
    for p in partners:
        pl.semaphore_signal(barrier, inc=1, device_id=p, device_id_type=MESH)

    sends = []

    def send(src, dst, ss, rs, dev):
        c = pltpu.make_async_remote_copy(
            src_ref=src, dst_ref=dst, send_sem=ss, recv_sem=rs, device_id=dev, device_id_type=MESH
        )
        c.start()
        sends.append(c)
        return c

    def window_x(ref, q):
        return ref.at[:, pl.ds(pl.multiple_of(q * wx, LANES), wx)]

    def window_y(ref, q):
        return ref.at[:, pl.ds(pl.multiple_of(base_y + q * wy, LANES), wy)]

    own_px = pltpu.make_async_copy(window_x(ptdf_ref, x), px.at[x], l_p.at[0])
    own_py = pltpu.make_async_copy(window_y(ptdf_ref, y), py.at[y], l_p.at[1])
    own_px.start()
    own_py.start()
    pl.semaphore_wait(barrier, len(partners))

    factor = []
    piece = ptdf_ref.shape[0] // PIECES

    def factor_piece(p):
        r = pl.ds(p * piece, piece)
        for k in range(1, NX):
            x_ = (x + k) % NX
            factor.append(send(
                ptdf_ref.at[r, pl.ds(pl.multiple_of(x_ * wx, LANES), wx)], px.at[x, r, :],
                s_p.at[k - 1, p], r_p.at[k - 1, p], at(z, y, x_),
            ))
        factor.append(send(
            ptdf_ref.at[r, pl.ds(pl.multiple_of(base_y + yother * wy, LANES), wy)], py.at[y, r, :],
            s_p.at[NX - 1, p], r_p.at[NX - 1, p], at(z, yother, x),
        ))

    col = plant_ref[...] - bus * (tiles * LANES)
    hi = col >> 7
    lo = col & 127
    row_id = lax.broadcasted_iota(jnp.int32, (2 * tiles, plants), 0)
    lo_id = lax.broadcasted_iota(jnp.int32, (LANES, plants), 0)
    lo_hot = (lo_id == lo).astype(jnp.float32).astype(jnp.bfloat16)
    eff = eff_ref[...]
    weight = rel_ref[...] * eff
    here = (row_id >> 1) == hi
    odd = (row_id & 1) == 1
    total = None
    for part in split3(weight):
        part = part.astype(jnp.float32)
        placed = jnp.where(here, jnp.where(odd, part[1:2, :], part[0:1, :]), 0.0)
        term = mm(placed.astype(jnp.bfloat16), lo_hot, NT)
        total = term if total is None else total + term
    acc[...] = total
    for h in range(tiles):
        cols = slice(h * LANES, (h + 1) * LANES)
        inj[:, cols] = (acc[2 * h : 2 * h + 2, :] + net_ref[:, cols].astype(jnp.float32)).astype(jnp.bfloat16)

    arrive_x, arrive_y = [], []
    for k, (dy, dx) in enumerate(xy_offsets):
        y_, x_ = xy(dy, dx)
        arrive_x.append(send(window_x(inj, x_), recv_in.at[me, :, pl.ds(0, wx)], s_i.at[2 * k], r_i.at[2 * k], at(z, y_, x_)))
    own_ix = pltpu.make_async_copy(window_x(inj, x), recv_in.at[me, :, pl.ds(0, wx)], l_i.at[0])
    own_ix.start()
    for k, (dy, dx) in enumerate(xy_offsets):
        y_, x_ = xy(dy, dx)
        arrive_y.append(send(window_y(inj, y_), recv_in.at[me, :, pl.ds(wx, wy)], s_i.at[2 * k + 1], r_i.at[2 * k + 1], at(z, y_, x_)))
    own_iy = pltpu.make_async_copy(window_y(inj, y), recv_in.at[me, :, pl.ds(wx, wy)], l_i.at[1])
    own_iy.start()
    factor_piece(0)

    cls = cls_ref[...]
    limit = jnp.zeros(cls.shape, jnp.float32)
    price = jnp.zeros(cls.shape, jnp.float32)
    for k in range(classes):
        limit = jnp.where(cls == k, lim_ref[k], limit)
        price = jnp.where(cls == k, price_ref[k], price)

    for s in range(2):
        hot[s] = jnp.where(here & (odd == (s == 1)), 1.0, 0.0).astype(jnp.bfloat16)
    flight = {}

    def ring_gather(step, d, c):
        start, size = chunks[c]
        if step > 1:
            flight[step - 1, d, c].wait_recv()
        n = (z + NZ - (step - 1)) % NZ if d == 0 else (z + (step - 1)) % NZ
        block = xall.at[n, :, pl.ds(start, size)]
        flight[step, d, c] = send(block, block, s_z.at[d, step - 1, c], r_z.at[d, step - 1, c], at(zup if d == 0 else zdn, y, x))

    own_ix.wait()
    for c in arrive_x:
        c.wait_recv()
    for i in range(NX * NY):
        xall[z, 2 * i : 2 * i + 2, 0:wx] = recv_in[i, :, 0:wx]
    for d in range(2):
        ring_gather(1, d, 0)
    own_iy.wait()
    for c in arrive_y:
        c.wait_recv()
    for i in range(NX * NY):
        xall[z, 2 * i : 2 * i + 2, wx:width] = recv_in[i, :, wx:width]
    for c in range(1, len(chunks)):
        for d in range(2):
            ring_gather(1, d, c)
    factor_piece(1)
    half = NZ // 2
    for step in range(2, half):
        for c in range(len(chunks)):
            for d in range(2):
                ring_gather(step, d, c)
        if step == 2:
            for p in range(2, PIECES):
                factor_piece(p)
    for c in range(len(chunks)):
        ring_gather(half, way[c], c)
    for c in range(len(chunks)):
        flight[half - 1, 1 - way[c], c].wait_recv()
        flight[half, way[c], c].wait_recv()

    own_px.wait()
    own_py.wait()
    for c in factor:
        c.wait_recv()
    scen = NZ * 2 * NX * NY
    lhs_x = xall[:, :, 0:wx].reshape(scen, wx)
    for q in range(NX):
        fpart[q] = mm(lhs_x, px[q], NT)
    lhs_y = xall[:, :, wx:width].reshape(scen, wy)
    for q in range(NY):
        fpart[NX + q] = mm(lhs_y, py[q], NT)

    def quarter(d):
        return pl.ds(pl.multiple_of((bus + d) % nbus * part_rows, part_rows), part_rows)

    slots = [(x + k) % NX for k in range(1, NX)] + [NX + yother, x]
    fpart[x] = fpart[x] + fpart[NX + y]
    back = []
    for j in range(NX + 1):
        for d in range(nbus):
            if (j, d) != (NX, 0):
                back.append(send(fpart.at[slots[j], quarter(d), :], frecv.at[j, d], s_f.at[j, d], r_f.at[j, d], across(j, d)))
    flows = fpart[x, quarter(0), :]
    for c in back:
        c.wait_recv()
    for j in range(NX + 1):
        for d in range(nbus):
            if (j, d) != (NX, 0):
                flows = flows + frecv[j, d]
    upper = jax.nn.sigmoid((flows - limit) / SMOOTH)
    lower = jax.nn.sigmoid((-flows - limit) / SMOOTH)
    gx[x, quarter(0), :] = (price * (upper - lower)).astype(jnp.bfloat16)
    given = []
    mine = gx.at[x, quarter(0), :]
    for j in range(NX + 1):
        for d in range(nbus):
            if (j, d) != (NX, 0):
                there = gy.at[y, quarter(0), :] if j == NX - 1 else mine
                given.append(send(mine, there, s_g.at[j, d], r_g.at[j, d], across(j, d)))
    for c in given:
        c.wait_recv()
    gy[y] = gx[x]

    def product(g, p, n):
        total = mm(g[0], p[0], NN)
        for q in range(1, n):
            total = total + mm(g[q], p[q], NN)
        return total.reshape(NZ, scen // NZ, p.shape[2])

    down = {}

    def ring_reduce(step, d, c):
        start, size = chunks[c]
        away = half + 1 - step
        target = (z + away) % NZ if d == 0 else (z + NZ - away) % NZ
        value = gpart[target, :, start : start + size]
        if (step - 1, d, c) in down:
            down[step - 1, d, c].wait_recv()
            value = value + ring[1, d, step - 2, :, start : start + size].astype(jnp.float32)
        ring[0, d, step - 1, :, start : start + size] = value.astype(jnp.bfloat16)
        down[step, d, c] = send(
            ring.at[0, d, step - 1, :, pl.ds(start, size)],
            ring.at[1, d, step - 1, :, pl.ds(start, size)],
            s_r.at[d, step - 1, c], r_r.at[d, step - 1, c],
            at(zup if d == 0 else zdn, y, x),
        )

    order = (1, 2, 3, 0)
    gpart[:, :, wx:width] = product(gy, py, NY)
    for c in order:
        if c == 0:
            gpart[:, :, 0:wx] = product(gx, px, NX)
        ring_reduce(1, way[c], c)
        ring_reduce(2, 1 - way[c], c)
    for c in order:
        ring_reduce(2, way[c], c)
    for step in range(3, half + 1):
        for c in order:
            ring_reduce(step, 1 - way[c], c)
        for c in order:
            ring_reduce(step, way[c], c)
    last = []
    for c in order:
        start, size = chunks[c]
        value = gpart[z, :, start : start + size]
        for d in range(2):
            down[half, d, c].wait_recv()
            value = value + ring[1, d, half - 1, :, start : start + size].astype(jnp.float32)
        for i in range(NX * NY):
            sbuf[i, :, start : start + size] = value[2 * i : 2 * i + 2, :]
        if c in (3, 0):
            start, size = (0, wx) if c == 0 else (wx, wy)
            for k, (dy, dx) in enumerate(xy_offsets):
                y2, x2 = xy(dy, dx)
                last.append(send(
                    sbuf.at[y2 * NX + x2, :, pl.ds(start, size)], srecv.at[me, :, pl.ds(start, size)],
                    s_s.at[k, c % 2], r_s.at[k, c % 2], at(z, y2, x2),
                ))
    srecv[me] = sbuf[me]
    for c in last:
        c.wait_recv()
    for q in range(NX):
        part = srecv[q, :, 0:wx]
        for j in range(1, NY):
            part = part + srecv[j * NX + q, :, 0:wx]
        gbus_ref[:, q * wx : (q + 1) * wx] = part
    for q in range(NY):
        part = srecv[q * NX, :, wx:width]
        for j in range(1, NX):
            part = part + srecv[q * NX + j, :, wx:width]
        gbus_ref[:, base_y + q * wy : base_y + (q + 1) * wy] = part

    for h in range(tiles):
        rows[2 * h : 2 * h + 2, :] = gbus_ref[:, h * LANES : (h + 1) * LANES]
    parts = jnp.concatenate(split3(rows[...]), axis=1)
    lo_mask = lo_id == lo
    for s in range(2):
        picked = mm(parts, hot[s], TN)
        picked = picked[0:LANES] + picked[LANES : 2 * LANES] + picked[2 * LANES :]
        picked = jnp.sum(jnp.where(lo_mask, picked, 0.0), axis=0, keepdims=True)
        prel[bus, s : s + 1, :] = picked * eff
    release = []
    for d in range(1, nbus):
        release.append(send(prel.at[bus], prel.at[bus], s_o.at[d - 1], r_o.at[d - 1], (br, (bus + d) % nbus)))
    for c in release:
        c.wait_recv()
    out = prel[0]
    for b in range(1, nbus):
        out = out + prel[b]
    grel_ref[...] = out
    for c in sends:
        c.wait_send()


def shards(net_load, release, plant_bus, efficiency, ptdf, branch_class, class_limit, class_price):
    nbus = 4
    plants = plant_bus.shape[0]
    classes = class_limit.shape[0]
    branches, columns = ptdf.shape
    tiles = columns // LANES
    tx = 15
    ty = (tiles - NX * tx) // NY
    wx, wy = tx * LANES, ty * LANES
    width = wx + wy
    group = NX * NY
    scen = NZ * group * 2
    bf, f32 = jnp.bfloat16, jnp.float32
    dma = pltpu.SemaphoreType.DMA
    vmem = pl.BlockSpec(memory_space=pltpu.VMEM)
    smem = pl.BlockSpec(memory_space=pltpu.SMEM)
    return pl.pallas_call(
        functools.partial(kernel, (tiles, tx, ty, nbus, plants, classes)),
        out_shape=(
            jax.ShapeDtypeStruct((2, columns), f32),
            jax.ShapeDtypeStruct((2, plants), f32),
        ),
        in_specs=[vmem, vmem, vmem, vmem, pl.BlockSpec(memory_space=pl.ANY), vmem, smem, smem],
        out_specs=(vmem, vmem),
        scratch_shapes=[
            pltpu.VMEM((2, columns), bf),
            pltpu.VMEM((2 * tiles, LANES), f32),
            pltpu.VMEM((NX, branches, wx), bf),
            pltpu.VMEM((NY, branches, wy), bf),
            pltpu.VMEM((group, 2, width), bf),
            pltpu.VMEM((NZ, 2 * group, width), bf),
            pltpu.VMEM((NX + NY, scen, branches), f32),
            pltpu.VMEM((NX + 1, nbus, scen // nbus, branches), f32),
            pltpu.VMEM((NX, scen, branches), bf),
            pltpu.VMEM((NY, scen, branches), bf),
            pltpu.VMEM((NZ, 2 * group, width), f32),
            pltpu.VMEM((2, 2, NZ // 2, 2 * group, width), bf),
            pltpu.VMEM((group, 2, width), f32),
            pltpu.VMEM((group, 2, width), f32),
            pltpu.VMEM((2 * tiles, LANES), f32),
            pltpu.VMEM((nbus, 2, plants), f32),
            pltpu.VMEM((2, 2 * tiles, plants), bf),
            dma((NX, PIECES)), dma((NX, PIECES)), dma((2,)),
            dma((2 * (group - 1),)), dma((2 * (group - 1),)), dma((2,)),
            dma((2, NZ // 2, 4)), dma((2, NZ // 2, 4)),
            dma((NX + 1, nbus)), dma((NX + 1, nbus)),
            dma((NX + 1, nbus)), dma((NX + 1, nbus)),
            dma((2, NZ // 2, 4)), dma((2, NZ // 2, 4)),
            dma((group - 1, 2)), dma((group - 1, 2)),
            dma((nbus - 1,)), dma((nbus - 1,)),
        ],
        compiler_params=pltpu.CompilerParams(
            collective_id=0, has_side_effects=True, vmem_limit_bytes=56 << 20
        ),
    )(
        net_load,
        release,
        plant_bus[None, :],
        efficiency[None, :],
        ptdf,
        branch_class[None, :],
        class_limit,
        class_price,
    )


def solution(mesh):
    placed = (P("br", "bus"), P("br", None), P(), P(), P("br", "bus"), P("br"), P(), P())
    return jax.shard_map(
        shards,
        mesh=mesh,
        in_specs=placed,
        out_specs=(P("br", "bus"), P("br", None)),
        check_vma=False,
    )
```

time: 93.4 us -> 83.9 us (0.90)
  Pallas kernels: 89.7 us -> 80.2 us
    pallas_call x1, Pallas kernels: 89.7 us -> 80.2 us  [shards(): pl.pallas_call(functools.partial(kernel, (tiles, tx, ty, nbus, plants, cl...]
where the time goes in v2:
time: 83.9 us; the launch traced here: 83.7 us
  Pallas kernels  80.2 us (96%)
  local copies, waits for them, and re-layouts  2.85 us (3%)
    pallas_call x1, Pallas kernels, shards(): pl.pallas_call(functools.partial(kernel, (tiles, tx, ty, nbus, plants, cl...  80.2 us
    unnamed x2, local copies, waits for them, and re-layouts  2.85 us

profile of v2, /device:TPU:1, one launch (start us, length us, event | category | flops | bytes accessed | tf_op | source)
XLA Modules:
  0.0 83.7 jit_solution(1749331770627820094)
XLA Ops:
  0.6 80.2 %shard_map.95 = (f32[2,15104]{1,0:T(2,128)}, f32[2,1024]{1,0:T(2,128)}) custom-call(bf16[2,15104]{1,0:T(2,128)(2,1)} %net_ref.1, f32[2,1024]{1,0:T(2,128)} %rel_ref.1, s32[1,1024]{1,0:T(1,128)} %bitcast.3, f32[1,1024]{1,0:T(1,128)} %bitcast.4, bf16[128,15104]{1,0:T(8,128)(2,1)} %ptdf_ref.1, s32[1,128]{1,0:T(1,128)} %bitcast.5, f32[16]{0:T(128)} %lim_ref.1, ...), custom_call_target="tpu_custom_call" | custom-call | tf_op jit(solution)/shard_map/pallas_call | solution.py:347
  80.8 1.6 %copy.12 = f32[2,15104]{1,0:T(2,128)} copy(f32[2,15104]{1,0:T(2,128)} %get-tuple-element.4) | data formatting | bytes 241664
  82.4 1.3 %copy.13 = f32[2,1024]{1,0:T(2,128)} copy(f32[2,1024]{1,0:T(2,128)} %get-tuple-element.5) | data formatting | bytes 16384

commit v3 on v2

--- a/solution.py
+++ b/solution.py
@@ -31,10 +31,11 @@
 
 def kernel(
     sizes,
-    net_ref, rel_ref, plant_ref, eff_ref, ptdf_ref, cls_ref, lim_ref, price_ref,
+    net_in, rel_in, plant_in, eff_in, ptdf_ref, cls_in, lim_in, price_in,
     gbus_ref, grel_ref,
+    net_ref, rel_ref, plant_ref, eff_ref, cls_ref, lim_ref, price_ref,
     inj, acc, px, py, recv_in, xall, fpart, frecv, gx, gy, gpart, ring, sbuf, srecv, rows, prel, hot,
-    s_p, r_p, l_p, s_i, r_i, l_i, s_z, r_z, s_f, r_f, s_g, r_g, s_r, r_r, s_s, r_s, s_o, r_o,
+    l_in, s_p, r_p, l_p, s_i, r_i, l_i, s_z, r_z, s_f, r_f, s_g, r_g, s_r, r_r, s_s, r_s, s_o, r_o,
 ):
     tiles, tx, ty, nbus, plants, classes = sizes
     wx, wy = tx * LANES, ty * LANES
@@ -73,6 +74,16 @@
     for p in partners:
         pl.semaphore_signal(barrier, inc=1, device_id=p, device_id_type=MESH)
 
+    loads = [
+        pltpu.make_async_copy(src, dst, l_in.at[i])
+        for i, (src, dst) in enumerate((
+            (plant_in, plant_ref), (rel_in, rel_ref), (eff_in, eff_ref), (net_in, net_ref),
+            (cls_in, cls_ref), (lim_in, lim_ref), (price_in, price_ref),
+        ))
+    ]
+    for c in loads:
+        c.start()
+
     sends = []
 
     def send(src, dst, ss, rs, dev):
@@ -93,8 +104,9 @@
     own_py = pltpu.make_async_copy(window_y(ptdf_ref, y), py.at[y], l_p.at[1])
     own_px.start()
     own_py.start()
-    pl.semaphore_wait(barrier, len(partners))
-
+
+    for c in loads:
+        c.wait()
     factor = []
     piece = ptdf_ref.shape[0] // PIECES
 
@@ -132,6 +144,7 @@
         cols = slice(h * LANES, (h + 1) * LANES)
         inj[:, cols] = (acc[2 * h : 2 * h + 2, :] + net_ref[:, cols].astype(jnp.float32)).astype(jnp.bfloat16)
 
+    pl.semaphore_wait(barrier, len(partners))
     arrive_x, arrive_y = [], []
     for k, (dy, dx) in enumerate(xy_offsets):
         y_, x_ = xy(dy, dx)
@@ -149,8 +162,8 @@
     limit = jnp.zeros(cls.shape, jnp.float32)
     price = jnp.zeros(cls.shape, jnp.float32)
     for k in range(classes):
-        limit = jnp.where(cls == k, lim_ref[k], limit)
-        price = jnp.where(cls == k, price_ref[k], price)
+        limit = jnp.where(cls == k, lim_ref[:, k : k + 1], limit)
+        price = jnp.where(cls == k, price_ref[:, k : k + 1], price)
 
     for s in range(2):
         hot[s] = jnp.where(here & (odd == (s == 1)), 1.0, 0.0).astype(jnp.bfloat16)
@@ -199,23 +212,30 @@
     for c in factor:
         c.wait_recv()
     scen = NZ * 2 * NX * NY
-    lhs_x = xall[:, :, 0:wx].reshape(scen, wx)
-    for q in range(NX):
-        fpart[q] = mm(lhs_x, px[q], NT)
-    lhs_y = xall[:, :, wx:width].reshape(scen, wy)
-    for q in range(NY):
-        fpart[NX + q] = mm(lhs_y, py[q], NT)
-
+    branches = ptdf_ref.shape[0]
+    scen = NZ * 2 * NX * NY
     def quarter(d):
         return pl.ds(pl.multiple_of((bus + d) % nbus * part_rows, part_rows), part_rows)
 
     slots = [(x + k) % NX for k in range(1, NX)] + [NX + yother, x]
-    fpart[x] = fpart[x] + fpart[NX + y]
     back = []
-    for j in range(NX + 1):
+
+    def to_holder(j):
         for d in range(nbus):
             if (j, d) != (NX, 0):
                 back.append(send(fpart.at[slots[j], quarter(d), :], frecv.at[j, d], s_f.at[j, d], r_f.at[j, d], across(j, d)))
+
+    part = mm(xall[:, :, 0:wx].reshape(scen, wx), px[...].reshape(NX * branches, wx), NT)
+    for q in range(NX):
+        fpart[q] = part[:, q * branches : (q + 1) * branches]
+    for j in range(NX - 1):
+        to_holder(j)
+    part = mm(xall[:, :, wx:width].reshape(scen, wy), py[...].reshape(NY * branches, wy), NT)
+    for q in range(NY):
+        fpart[NX + q] = part[:, q * branches : (q + 1) * branches]
+    to_holder(NX - 1)
+    fpart[x] = fpart[x] + fpart[NX + y]
+    to_holder(NX)
     flows = fpart[x, quarter(0), :]
     for c in back:
         c.wait_recv()
@@ -226,21 +246,21 @@
     upper = jax.nn.sigmoid((flows - limit) / SMOOTH)
     lower = jax.nn.sigmoid((-flows - limit) / SMOOTH)
     gx[x, quarter(0), :] = (price * (upper - lower)).astype(jnp.bfloat16)
-    given = []
+    given = {}
     mine = gx.at[x, quarter(0), :]
-    for j in range(NX + 1):
-        for d in range(nbus):
-            if (j, d) != (NX, 0):
-                there = gy.at[y, quarter(0), :] if j == NX - 1 else mine
-                given.append(send(mine, there, s_g.at[j, d], r_g.at[j, d], across(j, d)))
-    for c in given:
-        c.wait_recv()
+    for j in (NX, NX - 1, 0, 1, 2):
+        there = gy.at[y, quarter(0), :] if j == NX - 1 else mine
+        given[j] = [
+            send(mine, there, s_g.at[j, d], r_g.at[j, d], across(j, d)) for d in range(nbus) if (j, d) != (NX, 0)
+        ]
+    for j in (NX, NX - 1):
+        for c in given[j]:
+            c.wait_recv()
     gy[y] = gx[x]
 
     def product(g, p, n):
-        total = mm(g[0], p[0], NN)
-        for q in range(1, n):
-            total = total + mm(g[q], p[q], NN)
+        lhs = jnp.concatenate([g[q] for q in range(n)], axis=1)
+        total = mm(lhs, p[...].reshape(n * branches, p.shape[2]), NN)
         return total.reshape(NZ, scen // NZ, p.shape[2])
 
     down = {}
@@ -265,6 +285,9 @@
     gpart[:, :, wx:width] = product(gy, py, NY)
     for c in order:
         if c == 0:
+            for j in range(NX - 1):
+                for arrived in given[j]:
+                    arrived.wait_recv()
             gpart[:, :, 0:wx] = product(gx, px, NX)
         ring_reduce(1, way[c], c)
         ring_reduce(2, 1 - way[c], c)
@@ -293,27 +316,36 @@
                     s_s.at[k, c % 2], r_s.at[k, c % 2], at(z, y2, x2),
                 ))
     srecv[me] = sbuf[me]
-    for c in last:
+
+    def pick(first, count):
+        for h in range(first, first + count):
+            rows[2 * h : 2 * h + 2, :] = gbus_ref[:, h * LANES : (h + 1) * LANES]
+        parts = jnp.concatenate(split3(rows[2 * first : 2 * (first + count), :]), axis=1)
+        both = []
+        for s in range(2):
+            picked = mm(parts, hot[s, 2 * first : 2 * (first + count), :], TN)
+            both.append(picked[0:LANES] + picked[LANES : 2 * LANES] + picked[2 * LANES :])
+        return both
+
+    for c in last[: NX * NY - 1]:
+        c.wait_recv()
+    for q in range(NY):
+        part = srecv[q * NX, :, wx:width]
+        for j in range(1, NX):
+            part = part + srecv[q * NX + j, :, wx:width]
+        gbus_ref[:, base_y + q * wy : base_y + (q + 1) * wy] = part
+    picked_y = pick(NX * tx, NY * ty)
+    for c in last[NX * NY - 1 :]:
         c.wait_recv()
     for q in range(NX):
         part = srecv[q, :, 0:wx]
         for j in range(1, NY):
             part = part + srecv[j * NX + q, :, 0:wx]
         gbus_ref[:, q * wx : (q + 1) * wx] = part
-    for q in range(NY):
-        part = srecv[q * NX, :, wx:width]
-        for j in range(1, NX):
-            part = part + srecv[q * NX + j, :, wx:width]
-        gbus_ref[:, base_y + q * wy : base_y + (q + 1) * wy] = part
-
-    for h in range(tiles):
-        rows[2 * h : 2 * h + 2, :] = gbus_ref[:, h * LANES : (h + 1) * LANES]
-    parts = jnp.concatenate(split3(rows[...]), axis=1)
+    picked_x = pick(0, NX * tx)
     lo_mask = lo_id == lo
     for s in range(2):
-        picked = mm(parts, hot[s], TN)
-        picked = picked[0:LANES] + picked[LANES : 2 * LANES] + picked[2 * LANES :]
-        picked = jnp.sum(jnp.where(lo_mask, picked, 0.0), axis=0, keepdims=True)
+        picked = jnp.sum(jnp.where(lo_mask, picked_x[s] + picked_y[s], 0.0), axis=0, keepdims=True)
         prel[bus, s : s + 1, :] = picked * eff
     release = []
     for d in range(1, nbus):
@@ -326,6 +358,11 @@
     grel_ref[...] = out
     for c in sends:
         c.wait_send()
+
+
+def finish(gbus_in, grel_in, gbus_ref, grel_ref):
+    gbus_ref[...] = gbus_in[...]
+    grel_ref[...] = grel_in[...]
 
 
 def shards(net_load, release, plant_bus, efficiency, ptdf, branch_class, class_limit, class_price):
@@ -343,16 +380,22 @@
     bf, f32 = jnp.bfloat16, jnp.float32
     dma = pltpu.SemaphoreType.DMA
     vmem = pl.BlockSpec(memory_space=pltpu.VMEM)
-    smem = pl.BlockSpec(memory_space=pltpu.SMEM)
-    return pl.pallas_call(
+    out = pl.pallas_call(
         functools.partial(kernel, (tiles, tx, ty, nbus, plants, classes)),
         out_shape=(
             jax.ShapeDtypeStruct((2, columns), f32),
             jax.ShapeDtypeStruct((2, plants), f32),
         ),
-        in_specs=[vmem, vmem, vmem, vmem, pl.BlockSpec(memory_space=pl.ANY), vmem, smem, smem],
+        in_specs=[pl.BlockSpec(memory_space=pl.ANY)] * 8,
         out_specs=(vmem, vmem),
         scratch_shapes=[
+            pltpu.VMEM((2, columns), bf),
+            pltpu.VMEM((2, plants), f32),
+            pltpu.VMEM((1, plants), jnp.int32),
+            pltpu.VMEM((1, plants), f32),
+            pltpu.VMEM((1, branches), jnp.int32),
+            pltpu.VMEM((1, classes), f32),
+            pltpu.VMEM((1, classes), f32),
             pltpu.VMEM((2, columns), bf),
             pltpu.VMEM((2 * tiles, LANES), f32),
             pltpu.VMEM((NX, branches, wx), bf),
@@ -370,7 +413,7 @@
             pltpu.VMEM((2 * tiles, LANES), f32),
             pltpu.VMEM((nbus, 2, plants), f32),
             pltpu.VMEM((2, 2 * tiles, plants), bf),
-            dma((NX, PIECES)), dma((NX, PIECES)), dma((2,)),
+            dma((7,)), dma((NX, PIECES)), dma((NX, PIECES)), dma((2,)),
             dma((2 * (group - 1),)), dma((2 * (group - 1),)), dma((2,)),
             dma((2, NZ // 2, 4)), dma((2, NZ // 2, 4)),
             dma((NX + 1, nbus)), dma((NX + 1, nbus)),
@@ -389,9 +432,15 @@
         efficiency[None, :],
         ptdf,
         branch_class[None, :],
-        class_limit,
-        class_price,
+        class_limit[None, :],
+        class_price[None, :],
     )
+    return pl.pallas_call(
+        finish,
+        out_shape=(jax.ShapeDtypeStruct((2, columns), f32), jax.ShapeDtypeStruct((2, plants), f32)),
+        in_specs=[vmem] * 2,
+        out_specs=(vmem, vmem),
+    )(*out)
 
 
 def solution(mesh):

time: 83.9 us -> 79.7 us (0.950)
  local copies, waits for them, and re-layouts: 2.85 us -> 0 us
  Pallas kernels: 80.2 us -> 79 us
    unnamed x2 -> x0, local copies, waits for them, and re-layouts: 2.85 us -> none
    pallas_call x1, Pallas kernels: 80.2 us -> 77.4 us  [shards(): pl.pallas_call(functools.partial(kernel, (tiles, tx, ty, nbus, plants, cl...]
    pallas_call x0 -> x1, Pallas kernels: none -> 1.56 us  [shards(): pl.pallas_call(finish, out_shape=(jax.ShapeDtypeStruct((2, columns), f32)...]
where the time goes in v3:
time: 79.7 us; the launch traced here: 79.6 us
  Pallas kernels  79 us (99%)
    pallas_call x1, Pallas kernels, shards(): pl.pallas_call(functools.partial(kernel, (tiles, tx, ty, nbus, plants, cl...  77.4 us

profile of v3, /device:TPU:1, one launch (start us, length us, event | category | flops | bytes accessed | tf_op | source)
XLA Modules:
  0.0 79.6 jit_solution(13946865668823076990)
XLA Ops:
  0.6 77.4 %shard_map.95 = (f32[2,15104]{1,0:T(2,128)}, f32[2,1024]{1,0:T(2,128)}) custom-call(bf16[2,15104]{1,0:T(2,128)(2,1)} %net_in.1, f32[2,1024]{1,0:T(2,128)} %rel_in.1, s32[1,1024]{1,0:T(1,128)} %bitcast.5, f32[1,1024]{1,0:T(1,128)} %bitcast.6, bf16[128,15104]{1,0:T(8,128)(2,1)} %ptdf_ref.1, s32[1,128]{1,0:T(1,128)} %bitcast.7, f32[1,16]{1,0:T(1,128)} %bitcast.8, ...), custom_call_target="tpu_custom_call" | custom-call | tf_op jit(solution)/shard_map/pallas_call | solution.py:383
  78.0 1.6 %shard_map.96 = (f32[2,15104]{1,0:T(2,128)}, f32[2,1024]{1,0:T(2,128)}) custom-call(f32[2,15104]{1,0:T(2,128)} %get-tuple-element.4.gbus_in, f32[2,1024]{1,0:T(2,128)} %get-tuple-element.5.grel_in), custom_call_target="tpu_custom_call" | custom-call | tf_op jit(solution)/shard_map/pallas_call | solution.py:438

commit v4 on v3

--- a/solution.py
+++ b/solution.py
@@ -44,7 +44,7 @@
     part_rows = 2 * NZ * NX * NY // nbus
     third = (ty + 2) // 3 * LANES
     chunks = ((0, wx), (wx, third), (wx + third, third), (wx + 2 * third, wy - 2 * third))
-    way = (0, 1, 1, 0)
+    way = (1, 0, 0, 1)
     br, bus = lax.axis_index("br"), lax.axis_index("bus")
     z, y, x = br // (NX * NY), (br // NX) % NY, br % NX
     me = y * NX + x
@@ -112,7 +112,7 @@
 
     def factor_piece(p):
         r = pl.ds(p * piece, piece)
-        for k in range(1, NX):
+        for k in (2, 1, 3):
             x_ = (x + k) % NX
             factor.append(send(
                 ptdf_ref.at[r, pl.ds(pl.multiple_of(x_ * wx, LANES), wx)], px.at[x, r, :],

time: 79.7 us -> 78.8 us (0.989)
  Pallas kernels: 79 us -> 78 us
    pallas_call x1, Pallas kernels: 77.4 us -> 76.5 us  [shards(): pl.pallas_call(functools.partial(kernel, (tiles, tx, ty, nbus, plants, cl...]
where the time goes in v4:
time: 78.8 us; the launch traced here: 78.7 us
  Pallas kernels  78 us (99%)
    pallas_call x1, Pallas kernels, shards(): pl.pallas_call(functools.partial(kernel, (tiles, tx, ty, nbus, plants, cl...  76.5 us

profile of v4, /device:TPU:1, one launch (start us, length us, event | category | flops | bytes accessed | tf_op | source)
XLA Modules:
  0.0 78.7 jit_solution(613095587788638123)
XLA Ops:
  0.6 76.5 %shard_map.95 = (f32[2,15104]{1,0:T(2,128)}, f32[2,1024]{1,0:T(2,128)}) custom-call(bf16[2,15104]{1,0:T(2,128)(2,1)} %net_in.1, f32[2,1024]{1,0:T(2,128)} %rel_in.1, s32[1,1024]{1,0:T(1,128)} %bitcast.5, f32[1,1024]{1,0:T(1,128)} %bitcast.6, bf16[128,15104]{1,0:T(8,128)(2,1)} %ptdf_ref.1, s32[1,128]{1,0:T(1,128)} %bitcast.7, f32[1,16]{1,0:T(1,128)} %bitcast.8, ...), custom_call_target="tpu_custom_call" | custom-call | tf_op jit(solution)/shard_map/pallas_call | solution.py:383
  77.1 1.6 %shard_map.96 = (f32[2,15104]{1,0:T(2,128)}, f32[2,1024]{1,0:T(2,128)}) custom-call(f32[2,15104]{1,0:T(2,128)} %get-tuple-element.4.gbus_in, f32[2,1024]{1,0:T(2,128)} %get-tuple-element.5.grel_in), custom_call_target="tpu_custom_call" | custom-call | tf_op jit(solution)/shard_map/pallas_call | solution.py:438

commit v5 on v4

--- a/solution.py
+++ b/solution.py
@@ -248,7 +248,7 @@
     gx[x, quarter(0), :] = (price * (upper - lower)).astype(jnp.bfloat16)
     given = {}
     mine = gx.at[x, quarter(0), :]
-    for j in (NX, NX - 1, 0, 1, 2):
+    for j in (NX - 1, 1, 0, 2, NX):
         there = gy.at[y, quarter(0), :] if j == NX - 1 else mine
         given[j] = [
             send(mine, there, s_g.at[j, d], r_g.at[j, d], across(j, d)) for d in range(nbus) if (j, d) != (NX, 0)

time: 78.8 us -> 78.6 us (level)
  no operation moved by 1% of the time
where the time goes in v5:
time: 78.6 us; the launch traced here: 78.5 us
  Pallas kernels  77.8 us (99%)
    pallas_call x1, Pallas kernels, shards(): pl.pallas_call(functools.partial(kernel, (tiles, tx, ty, nbus, plants, cl...  76.3 us

profile of v5, /device:TPU:1, one launch (start us, length us, event | category | flops | bytes accessed | tf_op | source)
XLA Modules:
  0.0 78.5 jit_solution(4358688278301296510)
XLA Ops:
  0.6 76.3 %shard_map.95 = (f32[2,15104]{1,0:T(2,128)}, f32[2,1024]{1,0:T(2,128)}) custom-call(bf16[2,15104]{1,0:T(2,128)(2,1)} %net_in.1, f32[2,1024]{1,0:T(2,128)} %rel_in.1, s32[1,1024]{1,0:T(1,128)} %bitcast.5, f32[1,1024]{1,0:T(1,128)} %bitcast.6, bf16[128,15104]{1,0:T(8,128)(2,1)} %ptdf_ref.1, s32[1,128]{1,0:T(1,128)} %bitcast.7, f32[1,16]{1,0:T(1,128)} %bitcast.8, ...), custom_call_target="tpu_custom_call" | custom-call | tf_op jit(solution)/shard_map/pallas_call | solution.py:383
  76.9 1.6 %shard_map.96 = (f32[2,15104]{1,0:T(2,128)}, f32[2,1024]{1,0:T(2,128)}) custom-call(f32[2,15104]{1,0:T(2,128)} %get-tuple-element.4.gbus_in, f32[2,1024]{1,0:T(2,128)} %get-tuple-element.5.grel_in), custom_call_target="tpu_custom_call" | custom-call | tf_op jit(solution)/shard_map/pallas_call | solution.py:438
